TPU v7x, 256 devices: a whole 4x4x8 slice. The times are simulated.
256 devices in a mesh: rep: 128 (over z, y, x_hi, core), shard: 2 (over x_lo).
Axes of the slice: x: 4 (x_hi: 2, x_lo: 2; x = x_hi * 2 + x_lo), y: 4, z: 8, core: 2. Of those that a mesh axis runs over, the one named last changes fastest.
Arguments:
- grads: float32 [128, 4, 384, 1536], P('rep', None, 'shard'), may hold values from -6 to 6
- basis: float32 [4, 384, 128], P(None, 'shard'), may hold values from -0.3125 to 0.3125
- weights: float32 [4, 384, 1536], P(None, 'shard'), may hold values from -0.3125 to 0.3125
- first_moment: float32 [4, 128, 1536], P(None, 'shard'), may hold values from -6 to 6
- second_moment: float32 [4, 128, 1536], P(None, 'shard'), may hold values from 0.01 to 1
Outputs:
- new_weights: float32 [4, 384, 1536], P(None, 'shard')
- new_first: float32 [4, 128, 1536], P(None, 'shard')
- new_second: float32 [4, 128, 1536], P(None, 'shard')
- new_basis: float32 [4, 384, 128], P(None, 'shard')
All inputs are finite; a program needn't handle non-finite values.
Results may differ from a plain program's by a relative error of at most 0.000057.
Values sent between devices are 32-bit elements; how exact they have to be, the bound alone decides.
No kernel may reach another device: no remote copies, remote signals or barrier semaphores. Data moves between devices by JAX's collectives and lax.ppermute only.
A program may use at most 128 MiB of HBM per device.

v0:
```python
import jax
import jax.numpy as jnp
from jax import lax
from jax.sharding import Mesh, PartitionSpec as P

ADAM_STEP = 100
HIGH = lax.Precision.HIGHEST
SIZES = {"z": 8, "y": 4, "xh": 2, "core": 2, "xl": 2}
REP = ("z", "y", "xh", "core")


def shift(x, axis, k):
    n = SIZES[axis]
    return lax.ppermute(x, axis, [(i, (i + k) % n) for i in range(n)])


def flip(x, axis, bit=1):
    n = SIZES[axis]
    return lax.ppermute(x, axis, [(i, i ^ bit) for i in range(n)])


def rows(x, index, count):
    return lax.dynamic_slice_in_dim(x, index * count, count, 0)


def in_order(index, mine, other):
    first = index == 0
    return (jnp.where(first, mine, other), jnp.where(first, other, mine))


def scatter_direct(x, axis):
    n, me = (SIZES[axis], lax.axis_index(axis))
    count = x.shape[0] // n
    total = rows(x, me, count)
    for k in range(1, n):
        total = total + shift(rows(x, (me + k) % n, count), axis, k)
    return total


def gather_direct(x, axis):
    n, me = (SIZES[axis], lax.axis_index(axis))
    count = x.shape[0]
    out = jnp.zeros((n * count,) + x.shape[1:], x.dtype)
    out = lax.dynamic_update_slice_in_dim(out, x, me * count, 0)
    for k in range(1, n):
        out = lax.dynamic_update_slice_in_dim(out, shift(x, axis, k), (me - k) % n * count, 0)
    return out


def scatter_exchange(x, axis):
    n = SIZES[axis]
    parts = x.reshape((n, x.shape[0] // n) + x.shape[1:])
    return jnp.sum(lax.all_to_all(parts, axis, split_axis=0, concat_axis=0), axis=0)


def on_device(grads, basis, weights, first_moment, second_moment):
    layers, depth, width = grads.shape[1:]
    rank = basis.shape[2]
    half = layers // 2
    piece = width // 64
    z, y, xh = (lax.axis_index("z"), lax.axis_index("y"), lax.axis_index("xh"))
    core, xl = (lax.axis_index("core"), lax.axis_index("xl"))
    place = (y * 2 + xh) * 8 + z
    given = flip(rows(grads[0], 1 - core, half), "core")
    pair = rows(grads[0], core, half) + given
    held = pair.reshape(half * depth, width).T
    held = scatter_direct(held, "y")
    held = scatter_direct(held, "xh")
    total = scatter_exchange(held, "z").reshape(piece, half, depth)
    basis_pair = rows(basis, core, half)
    cut = [
        jnp.swapaxes(
            lax.dynamic_slice(m, (core * half, 0, place * piece), (half, rank // 2, piece)), 1, 2
        )
        for m in (first_moment, second_moment)
    ]
    cut = jnp.concatenate(cut, axis=2)
    low, high = in_order(xl, cut, flip(cut, "xl"))
    first = jnp.concatenate([low[:, :, : rank // 2], high[:, :, : rank // 2]], axis=2)
    second = jnp.concatenate([low[:, :, rank // 2 :], high[:, :, rank // 2 :]], axis=2)
    proj = jnp.einsum("fld,ldr->lfr", total, basis_pair, precision=HIGH)
    proj = proj + flip(proj, "xl")
    new_first = 0.9 * first + 0.1 * proj
    new_second = 0.999 * second + 0.001 * proj * proj
    direction = (
        new_first
        / (1.0 - 0.9**ADAM_STEP)
        / (jnp.sqrt(new_second / (1.0 - 0.999**ADAM_STEP)) + 1e-08)
    )
    mine = jnp.where(xl == 0, proj[:, :, : rank // 2], proj[:, :, rank // 2 :])
    packed = jnp.concatenate([direction[0], direction[1], mine[0], mine[1]], axis=1)
    refresh = jnp.einsum("fld,lfr->ldr", total, proj, precision=HIGH)
    part = scatter_exchange(refresh.reshape(half * depth, rank), "z")
    part = part + flip(part, "y", 1)
    part = part + flip(part, "y", 2)
    part = part + flip(part, "xh")
    refresh = lax.all_gather(part, "z", axis=0, tiled=True).reshape(half, depth, rank)
    gram = jnp.einsum("ldr,lds->lrs", refresh, refresh, precision=HIGH)
    gram = gram + flip(gram, "xl")
    sumsq = jnp.einsum("lrr->l", gram)
    factor = jnp.sqrt(jnp.float32(rank)) / (2.0 * jnp.sqrt(sumsq + 1e-06))
    scaled = refresh * factor[:, None, None]
    gram_scaled = gram * (factor * factor)[:, None, None]
    basis_new = 1.5 * scaled - 0.5 * jnp.einsum("ldr,lrs->lds", scaled, gram_scaled, precision=HIGH)
    new_basis = jnp.concatenate(in_order(core, basis_new, flip(basis_new, "core")), axis=0)
    packed = lax.all_gather(packed, "z", axis=0, tiled=True)
    packed = gather_direct(packed, "xh")
    packed = gather_direct(packed, "y")
    packed = jnp.stack(in_order(core, packed, flip(packed, "core")))
    dirs = packed[:, :, : half * rank].reshape(2, width, half, rank)
    own = packed[:, :, half * rank :].reshape(2, width, half, rank // 2)
    own = jnp.transpose(own, (0, 2, 3, 1)).reshape(layers, rank // 2, width)
    new_first = 0.9 * first_moment + 0.1 * own
    new_second = 0.999 * second_moment + 0.001 * own * own
    dirs = jnp.transpose(dirs, (0, 2, 1, 3)).reshape(layers, width, rank)
    update = jnp.einsum("ldr,lfr->ldf", basis, dirs, precision=HIGH)
    new_weights = weights - 0.0125 * update
    return (new_weights, new_first, new_second, new_basis)


def solution(mesh):
    fine = Mesh(mesh.devices.reshape(8, 4, 2, 2, 2), ("z", "y", "xh", "core", "xl"))
    split = P(None, "xl", None)
    return jax.shard_map(
        on_device,
        mesh=fine,
        in_specs=(P(REP, None, "xl", None), split, split, split, split),
        out_specs=(split, split, split, split),
        check_vma=False,
    )
```

profile of v0, /device:TPU:1, one launch (start us, length us, event | category | flops | bytes accessed | tf_op | source)
XLA Modules:
  0.0 224.6 jit_solution(4249226077808333504)
XLA Ops:
  0.7 1.9 dynamic-slice_bitcast_fusion
  2.5 3.3 %collective-permute-start.1 = (f32[2,192,1536]{2,1,0:T(8,128)S(1)}, f32[2,192,1536]{2,1,0:T(8,128)}, u32[]{:S(2)}, u32[]{:S(2)}) collective-permute-start(f32[2,192,1536]{2,1,0:T(8,128)S(1)} %dynamic-slice_bitcast_fusion), channel_id=1, source_target_pairs={{0,2},{2,0},{1,3},{3,1},{4,6},{6,4},{5,7},{7,5},{8,10},{10,8},{9,1... | collective-permute-start | bytes 7077896 | tf_op jit(solution)/shard_map/ppermute | solution.py:19
  5.9 4.3 %collective-permute-done.1 = f32[2,192,1536]{2,1,0:T(8,128)} collective-permute-done((f32[2,192,1536]{2,1,0:T(8,128)S(1)}, f32[2,192,1536]{2,1,0:T(8,128)}, u32[]{:S(2)}, u32[]{:S(2)}) %collective-permute-start.1) | collective-permute-done | bytes 2359328 | tf_op jit(solution)/shard_map/ppermute | solution.py:19
  10.1 2.8 %bitcast_add_fusion = f32[2,192,1536]{2,1,0:T(8,128)S(1)} fusion(f32[2,192,1536]{2,1,0:T(8,128)} %collective-permute-done.1, f32[1,4,192,1536]{3,2,1,0:T(8,128)} %param.5, s32[]{:T(128)S(6)} %select_n.129), kind=kLoop, calls=%fused_computation.7 | loop fusion | flops 589824 | bytes 7077892 | tf_op jit(solution)/shard_map/add | solution.py:65
  16.1 12.8 %collective-permute-done.4 = f32[384,384]{0,1:T(8,128)} collective-permute-done((f32[384,384]{0,1:T(8,128)}, f32[384,384]{0,1:T(8,128)}, u32[]{:S(2)}, u32[]{:S(2)}) %collective-permute-start.4) | collective-permute-done | bytes 589856 | tf_op jit(solution)/shard_map/ppermute | solution.py:14
  28.9 2.3 %collective-permute-done.3 = f32[384,384]{0,1:T(8,128)} collective-permute-done((f32[384,384]{0,1:T(8,128)}, f32[384,384]{0,1:T(8,128)}, u32[]{:S(2)}, u32[]{:S(2)}) %collective-permute-start.3) | collective-permute-done | bytes 589856 | tf_op jit(solution)/shard_map/ppermute | solution.py:14
  31.2 13.3 %collective-permute-done.2 = f32[384,384]{0,1:T(8,128)} collective-permute-done((f32[384,384]{0,1:T(8,128)S(1)}, f32[384,384]{0,1:T(8,128)}, u32[]{:S(2)}, u32[]{:S(2)}) %collective-permute-start.2) | collective-permute-done | bytes 589856 | tf_op jit(solution)/shard_map/ppermute | solution.py:14
  44.5 1.5 fusion.4
  46.2 2.8 %collective-permute-start.5 = (f32[192,384]{0,1:T(8,128)S(1)}, f32[192,384]{0,1:T(8,128)S(1)}, u32[]{:S(2)}, u32[]{:S(2)}) collective-permute-start(f32[192,384]{0,1:T(8,128)S(1)} %constant_dynamic-slice_fusion), channel_id=1, source_target_pairs={{0,4},{4,0},{1,5},{5,1},{2,6},{6,2},{3,7},{7,3},{8,12},{12,8},{9,1... | collective-permute-start | bytes 884744 | tf_op jit(solution)/shard_map/ppermute | solution.py:14
  50.3 7.6 %collective-permute-done.5 = f32[192,384]{0,1:T(8,128)S(1)} collective-permute-done((f32[192,384]{0,1:T(8,128)S(1)}, f32[192,384]{0,1:T(8,128)S(1)}, u32[]{:S(2)}, u32[]{:S(2)}) %collective-permute-start.5) | collective-permute-done | bytes 294944 | tf_op jit(solution)/shard_map/ppermute | solution.py:14
  58.9 8.2 %all-to-all-start = ((f32[8,24,384]{2,1,0:T(8,128)}), f32[8,24,384]{2,1,0:T(8,128)S(1)}, u32[]{:S(2)}, u32[]{:S(2)}) async-start(f32[8,24,384]{2,1,0:T(8,128)} %bitcast.9), calls=%async_computation | async-start | bytes 589824 | tf_op jit(solution)/shard_map/all_to_all | solution.py:53
  68.4 1.5 collective-permute-done
  70.0 7.4 %all-to-all-done = f32[8,24,384]{2,1,0:T(8,128)S(1)} async-done(((f32[8,24,384]{2,1,0:T(8,128)}), f32[8,24,384]{2,1,0:T(8,128)S(1)}, u32[]{:S(2)}, u32[]{:S(2)}) %all-to-all-start) | async-done | bytes 294944 | tf_op jit(solution)/shard_map/all_to_all | solution.py:53
  80.8 18.8 %all_gather.6 = f32[192,384]{1,0:T(8,128)S(1)} all-gather(f32[24,384]{1,0:T(8,128)S(1)} %pad_maximum_fusion.3), channel_id=1, replica_groups=mesh['z'=8,'y'=4,'xh'=2,'core'=2,'xl'=2] {'z'}, dimensions={0}, use_global_device_ids=true | all-gather | bytes 331776 | tf_op jit(solution)/shard_map/all_gather | solution.py:106
  99.6 2.7 %collective-permute-start.7 = (f32[192,384]{1,0:T(8,128)S(1)}, f32[192,384]{1,0:T(8,128)S(1)}, u32[]{:S(2)}, u32[]{:S(2)}) collective-permute-start(f32[192,384]{1,0:T(8,128)S(1)} %all_gather.6), channel_id=1, source_target_pairs={{0,4},{4,0},{1,5},{5,1},{2,6},{6,2},{3,7},{7,3},{8,12},{12,8},{9,1... | collective-permute-start | bytes 884744 | tf_op jit(solution)/shard_map/ppermute | solution.py:14
  102.5 3.5 %dynamic_update_slice.18 = f32[384,384]{0,1:T(8,128)S(1)} dynamic-update-slice(f32[384,384]{0,1:T(8,128)S(1)} %broadcast_in_dim.15, f32[192,384]{0,1:T(8,128)S(1)} %copy.23, s32[]{:T(128)S(6)} %select_n.141, s32[]{:T(128)} %constant.94.clone.1) | dynamic-update-slice | bytes 589828 | tf_op jit(solution)/shard_map/dynamic_update_slice | solution.py:44
  106.8 3.4 %dynamic_update_slice.19 = f32[384,384]{0,1:T(8,128)S(1)} dynamic-update-slice(f32[384,384]{0,1:T(8,128)S(1)} %dynamic_update_slice.18, f32[192,384]{0,1:T(8,128)S(1)} %copy.24, s32[]{:T(128)S(6)} %select_n.147, s32[]{:T(128)} %constant.94.clone.1) | dynamic-update-slice | bytes 589828 | tf_op jit(solution)/shard_map/dynamic_update_slice | solution.py:46
  111.6 2.0 collective-permute-start.10
  114.0 13.3 %collective-permute-done.8 = f32[384,384]{0,1:T(8,128)} collective-permute-done((f32[384,384]{0,1:T(8,128)S(1)}, f32[384,384]{0,1:T(8,128)}, u32[]{:S(2)}, u32[]{:S(2)}) %collective-permute-start.8) | collective-permute-done | bytes 589856 | tf_op jit(solution)/shard_map/ppermute | solution.py:14
  130.7 13.0 %collective-permute-start.11 = (f32[1536,384]{0,1:T(8,128)S(1)}, f32[1536,384]{0,1:T(8,128)}, u32[]{:S(2)}, u32[]{:S(2)}) collective-permute-start(f32[1536,384]{0,1:T(8,128)S(1)} %constant_dynamic-update-slice_fusion), channel_id=1, source_target_pairs={{0,2},{2,0},{1,3},{3,1},{4,6},{6,4},{5,7},{7,5},{8,10},{10,8},{9,1... | collective-permute-start | bytes 7077896 | tf_op jit(solution)/shard_map/ppermute | solution.py:19
  144.2 13.6 %all_to_all.10 = f32[8,48,128]{2,1,0:T(8,128)S(1)} all-to-all(f32[8,48,128]{2,1,0:T(8,128)S(1)} %bitcast.53), channel_id=1, replica_groups=mesh['z'=8,'y'=4,'xh'=2,'core'=2,'xl'=2] {'z'}, dimensions={0} | all-to-all | bytes 393216 | tf_op jit(solution)/shard_map/all_to_all | solution.py:53
  157.9 2.7 %collective-permute-done.12 = f32[48,128]{1,0:T(8,128)S(1)} collective-permute-done((f32[48,128]{1,0:T(8,128)S(1)}, f32[48,128]{1,0:T(8,128)S(1)}, u32[]{:S(2)}, u32[]{:S(2)}) %collective-permute-start.12) | collective-permute-done | bytes 24608 | tf_op jit(solution)/shard_map/ppermute | solution.py:19
  160.8 3.9 %collective-permute-done.13 = f32[48,128]{1,0:T(8,128)S(1)} collective-permute-done((f32[48,128]{1,0:T(8,128)S(1)}, f32[48,128]{1,0:T(8,128)S(1)}, u32[]{:S(2)}, u32[]{:S(2)}) %collective-permute-start.13) | collective-permute-done | bytes 24608 | tf_op jit(solution)/shard_map/ppermute | solution.py:19
  164.7 2.8 %collective-permute-start.14 = (f32[48,128]{1,0:T(8,128)S(1)}, f32[48,128]{1,0:T(8,128)S(1)}, u32[]{:S(2)}, u32[]{:S(2)}) collective-permute-start(f32[48,128]{1,0:T(8,128)S(1)} %add.190), channel_id=1, source_target_pairs={{0,4},{4,0},{1,5},{5,1},{2,6},{6,2},{3,7},{7,3},{8,12},{12,8},{9,1... | collective-permute-start | bytes 73736 | tf_op jit(solution)/shard_map/ppermute | solution.py:19
  168.9 18.6 %all_gather.7 = f32[384,128]{1,0:T(8,128)S(1)} all-gather(f32[48,128]{1,0:T(8,128)S(1)} %add.191), channel_id=1, replica_groups=mesh['z'=8,'y'=4,'xh'=2,'core'=2,'xl'=2] {'z'}, dimensions={0}, use_global_device_ids=true | all-gather | bytes 221184 | tf_op jit(solution)/shard_map/all_gather | solution.py:97
  189.6 2.9 %collective-permute-done.15 = f32[2,128,128]{2,1,0:T(8,128)S(1)} collective-permute-done((f32[2,128,128]{2,1,0:T(8,128)S(1)}, f32[2,128,128]{2,1,0:T(8,128)S(1)}, u32[]{:S(2)}, u32[]{:S(2)}) %collective-permute-start.15) | collective-permute-done | bytes 131104 | tf_op jit(solution)/shard_map/ppermute | solution.py:19
  193.0 11.1 %collective-permute-start.16 = (f32[2,192,128]{2,1,0:T(8,128)S(1)}, f32[2,192,128]{2,1,0:T(8,128)S(1)}, u32[]{:S(2)}, u32[]{:S(2)}) collective-permute-start(f32[2,192,128]{2,1,0:T(8,128)S(1)} %multiply_subtract_fusion), channel_id=1, source_target_pairs={{0,2},{2,0},{1,3},{3,1},{4,6},{6,4},{5,7},{7,5},{8,10},{10,8},{9,1... | collective-permute-start | bytes 589832 | tf_op jit(solution)/shard_map/ppermute | solution.py:19
  206.0 2.1 select_bitcast_fusion
  208.1 1.7 pad_maximum_fusion.1
  210.1 2.4 %copy.25 = f32[2,3072,128]{2,1,0:T(8,128)} copy(f32[2,3072,128]{1,2,0:T(8,128)S(1)} %pad_maximum_fusion) | data formatting | bytes 6291456 | tf_op jit(solution)/shard_map/concatenate
  212.4 4.9 %fusion = (f32[4,64,1536]{2,1,0:T(8,128)}, f32[4,64,1536]{2,1,0:T(8,128)}) fusion(f32[4,64,1536]{2,1,0:T(8,128)} %bitcast.50, f32[4,64,1536]{2,1,0:T(8,128)} %param.9, f32[4,64,1536]{2,1,0:T(8,128)} %param.8), kind=kLoop, calls=%fused_computation.11 | loop fusion | flops 2752512 | bytes 7864320 | tf_op jit(solution)/shard_map/add | solution.py:114
  217.3 7.3 %bitcast_subtract_fusion = f32[4,192,1536]{2,1,0:T(8,128)} fusion(f32[4,192,1536]{2,1,0:T(8,128)} %param.7, f32[4,1536,128]{2,1,0:T(8,128)S(1)} %bitcast.47, f32[4,192,128]{2,1,0:T(8,128)S(1)} %copy-done), kind=kOutput, calls=%fused_computation.4 | convolution fusion | flops 1814298624 | bytes 12976128 | tf_op jit(solution)/shard_map/ldr,lfr->ldf/dot_general | solution.py:116
  (61 shorter events, 23.5 us)
Async XLA Ops:
  0.6 76.8 %copy-start = (f32[4,192,128]{2,1,0:T(8,128)S(1)}, f32[4,192,128]{2,1,0:T(8,128)}, u32[]{:S(2)}) copy-start(f32[4,192,128]{2,1,0:T(8,128)} %param.6) | copy-start | bytes 1179652
  2.5 7.6 %collective-permute-start.1 = (f32[2,192,1536]{2,1,0:T(8,128)S(1)}, f32[2,192,1536]{2,1,0:T(8,128)}, u32[]{:S(2)}, u32[]{:S(2)}) collective-permute-start(f32[2,192,1536]{2,1,0:T(8,128)S(1)} %dynamic-slice_bitcast_fusion), channel_id=1, source_target_pairs={{0,2},{2,0},{1,3},{3,1},{4,6},{6,4},{5,7},{7,5},{8,10},{10,8},{9,1... | collective-permute-start | bytes 7077896 | tf_op jit(solution)/shard_map/ppermute | solution.py:19
  14.1 14.9 %collective-permute-start.4 = (f32[384,384]{0,1:T(8,128)}, f32[384,384]{0,1:T(8,128)}, u32[]{:S(2)}, u32[]{:S(2)}) collective-permute-start(f32[384,384]{0,1:T(8,128)} %get-tuple-element.16), channel_id=1, source_target_pairs={{0,24},{8,0},{16,8},{24,16},{1,25},{9,1},{17,9},{25,17},{2,26},{10... | collective-permute-start | bytes 1769480 | tf_op jit(solution)/shard_map/ppermute | solution.py:14
  15.1 16.1 %collective-permute-start.3 = (f32[384,384]{0,1:T(8,128)}, f32[384,384]{0,1:T(8,128)}, u32[]{:S(2)}, u32[]{:S(2)}) collective-permute-start(f32[384,384]{0,1:T(8,128)} %get-tuple-element.17), channel_id=1, source_target_pairs={{0,16},{8,24},{16,0},{24,8},{1,17},{9,25},{17,1},{25,9},{2,18},{10... | collective-permute-start | bytes 1769480 | tf_op jit(solution)/shard_map/ppermute | solution.py:14
  15.4 29.0 %collective-permute-start.2 = (f32[384,384]{0,1:T(8,128)S(1)}, f32[384,384]{0,1:T(8,128)}, u32[]{:S(2)}, u32[]{:S(2)}) collective-permute-start(f32[384,384]{0,1:T(8,128)S(1)} %get-tuple-element.15), channel_id=1, source_target_pairs={{0,8},{8,16},{16,24},{24,0},{1,9},{9,17},{17,25},{25,1},{2,10},{10... | collective-permute-start | bytes 1769480 | tf_op jit(solution)/shard_map/ppermute | solution.py:14
  46.2 11.6 %collective-permute-start.5 = (f32[192,384]{0,1:T(8,128)S(1)}, f32[192,384]{0,1:T(8,128)S(1)}, u32[]{:S(2)}, u32[]{:S(2)}) collective-permute-start(f32[192,384]{0,1:T(8,128)S(1)} %constant_dynamic-slice_fusion), channel_id=1, source_target_pairs={{0,4},{4,0},{1,5},{5,1},{2,6},{6,2},{3,7},{7,3},{8,12},{12,8},{9,1... | collective-permute-start | bytes 884744 | tf_op jit(solution)/shard_map/ppermute | solution.py:14
  58.9 18.5 %all-to-all-start = ((f32[8,24,384]{2,1,0:T(8,128)}), f32[8,24,384]{2,1,0:T(8,128)S(1)}, u32[]{:S(2)}, u32[]{:S(2)}) async-start(f32[8,24,384]{2,1,0:T(8,128)} %bitcast.9), calls=%async_computation | async-start | bytes 589824 | tf_op jit(solution)/shard_map/all_to_all | solution.py:53
  67.1 2.7 %collective-permute-start = (f32[2,24,128]{2,1,0:T(8,128)S(1)}, f32[2,24,128]{2,1,0:T(8,128)S(1)}, u32[]{:S(2)}, u32[]{:S(2)}) collective-permute-start(f32[2,24,128]{2,1,0:T(8,128)S(1)} %pad_maximum_fusion.4), channel_id=1, source_target_pairs={{0,1},{1,0},{2,3},{3,2},{4,5},{5,4},{6,7},{7,6},{8,9},{9,8},{10,11... | collective-permute-start | bytes 73736 | tf_op jit(solution)/shard_map/ppermute | solution.py:19
  77.8 2.8 %collective-permute-start.6 = (f32[2,24,128]{2,1,0:T(8,128)S(1)}, f32[2,24,128]{2,1,0:T(8,128)S(1)}, u32[]{:S(2)}, u32[]{:S(2)}) collective-permute-start(f32[2,24,128]{2,1,0:T(8,128)S(1)} %fusion.5), channel_id=1, source_target_pairs={{0,1},{1,0},{2,3},{3,2},{4,5},{5,4},{6,7},{7,6},{8,9},{9,8},{10,11... | collective-permute-start | bytes 73736 | tf_op jit(solution)/shard_map/ppermute | solution.py:19
  99.6 7.1 %collective-permute-start.7 = (f32[192,384]{1,0:T(8,128)S(1)}, f32[192,384]{1,0:T(8,128)S(1)}, u32[]{:S(2)}, u32[]{:S(2)}) collective-permute-start(f32[192,384]{1,0:T(8,128)S(1)} %all_gather.6), channel_id=1, source_target_pairs={{0,4},{4,0},{1,5},{5,1},{2,6},{6,2},{3,7},{7,3},{8,12},{12,8},{9,1... | collective-permute-start | bytes 884744 | tf_op jit(solution)/shard_map/ppermute | solution.py:14
  110.2 17.0 %collective-permute-start.8 = (f32[384,384]{0,1:T(8,128)S(1)}, f32[384,384]{0,1:T(8,128)}, u32[]{:S(2)}, u32[]{:S(2)}) collective-permute-start(f32[384,384]{0,1:T(8,128)S(1)} %dynamic_update_slice.19), channel_id=1, source_target_pairs={{0,8},{8,16},{16,24},{24,0},{1,9},{9,17},{17,25},{25,1},{2,10},{10... | collective-permute-start | bytes 1769480 | tf_op jit(solution)/shard_map/ppermute | solution.py:14
  110.3 18.1 %collective-permute-start.9 = (f32[384,384]{0,1:T(8,128)S(1)}, f32[384,384]{0,1:T(8,128)}, u32[]{:S(2)}, u32[]{:S(2)}) collective-permute-start(f32[384,384]{0,1:T(8,128)S(1)} %dynamic_update_slice.19), channel_id=1, source_target_pairs={{0,16},{8,24},{16,0},{24,8},{1,17},{9,25},{17,1},{25,9},{2,18},{10... | collective-permute-start | bytes 1769480 | tf_op jit(solution)/shard_map/ppermute | solution.py:14
  111.6 17.9 %collective-permute-start.10 = (f32[384,384]{0,1:T(8,128)S(1)}, f32[384,384]{0,1:T(8,128)}, u32[]{:S(2)}, u32[]{:S(2)}) collective-permute-start(f32[384,384]{0,1:T(8,128)S(1)} %dynamic_update_slice.19), channel_id=1, source_target_pairs={{0,24},{8,0},{16,8},{24,16},{1,25},{9,1},{17,9},{25,17},{2,26},{10... | collective-permute-start | bytes 1769480 | tf_op jit(solution)/shard_map/ppermute | solution.py:14
  130.7 75.3 %collective-permute-start.11 = (f32[1536,384]{0,1:T(8,128)S(1)}, f32[1536,384]{0,1:T(8,128)}, u32[]{:S(2)}, u32[]{:S(2)}) collective-permute-start(f32[1536,384]{0,1:T(8,128)S(1)} %constant_dynamic-update-slice_fusion), channel_id=1, source_target_pairs={{0,2},{2,0},{1,3},{3,1},{4,6},{6,4},{5,7},{7,5},{8,10},{10,8},{9,1... | collective-permute-start | bytes 7077896 | tf_op jit(solution)/shard_map/ppermute | solution.py:19
  157.8 2.8 %collective-permute-start.12 = (f32[48,128]{1,0:T(8,128)S(1)}, f32[48,128]{1,0:T(8,128)S(1)}, u32[]{:S(2)}, u32[]{:S(2)}) collective-permute-start(f32[48,128]{1,0:T(8,128)S(1)} %reduce_sum.28), channel_id=1, source_target_pairs={{0,8},{8,0},{16,24},{24,16},{1,9},{9,1},{17,25},{25,17},{2,10},{10... | collective-permute-start | bytes 73736 | tf_op jit(solution)/shard_map/ppermute | solution.py:19
  160.6 4.2 %collective-permute-start.13 = (f32[48,128]{1,0:T(8,128)S(1)}, f32[48,128]{1,0:T(8,128)S(1)}, u32[]{:S(2)}, u32[]{:S(2)}) collective-permute-start(f32[48,128]{1,0:T(8,128)S(1)} %add.189), channel_id=1, source_target_pairs={{0,16},{8,24},{16,0},{24,8},{1,17},{9,25},{17,1},{25,9},{2,18},{10... | collective-permute-start | bytes 73736 | tf_op jit(solution)/shard_map/ppermute | solution.py:19
  164.7 4.2 %collective-permute-start.14 = (f32[48,128]{1,0:T(8,128)S(1)}, f32[48,128]{1,0:T(8,128)S(1)}, u32[]{:S(2)}, u32[]{:S(2)}) collective-permute-start(f32[48,128]{1,0:T(8,128)S(1)} %add.190), channel_id=1, source_target_pairs={{0,4},{4,0},{1,5},{5,1},{2,6},{6,2},{3,7},{7,3},{8,12},{12,8},{9,1... | collective-permute-start | bytes 73736 | tf_op jit(solution)/shard_map/ppermute | solution.py:19
  188.2 4.2 %collective-permute-start.15 = (f32[2,128,128]{2,1,0:T(8,128)S(1)}, f32[2,128,128]{2,1,0:T(8,128)S(1)}, u32[]{:S(2)}, u32[]{:S(2)}) collective-permute-start(f32[2,128,128]{2,1,0:T(8,128)S(1)} %fusion.27), channel_id=1, source_target_pairs={{0,1},{1,0},{2,3},{3,2},{4,5},{5,4},{6,7},{7,6},{8,9},{9,8},{10,11... | collective-permute-start | bytes 393224 | tf_op jit(solution)/shard_map/ppermute | solution.py:19
  193.0 12.2 %collective-permute-start.16 = (f32[2,192,128]{2,1,0:T(8,128)S(1)}, f32[2,192,128]{2,1,0:T(8,128)S(1)}, u32[]{:S(2)}, u32[]{:S(2)}) collective-permute-start(f32[2,192,128]{2,1,0:T(8,128)S(1)} %multiply_subtract_fusion), channel_id=1, source_target_pairs={{0,2},{2,0},{1,3},{3,1},{4,6},{6,4},{5,7},{7,5},{8,10},{10,8},{9,1... | collective-permute-start | bytes 589832 | tf_op jit(solution)/shard_map/ppermute | solution.py:19
  212.4 4.9 %copy-start.1 = (f32[2,3072,128]{2,1,0:T(8,128)S(1)}, f32[2,3072,128]{2,1,0:T(8,128)}, u32[]{:S(2)}) copy-start(f32[2,3072,128]{2,1,0:T(8,128)} %copy.25) | copy-start | bytes 9437188
where the time goes:
time: 225 us
  waiting for transfers between devices  76.2 us (34%)
  starting transfers between devices  53.7 us (24%)
  blocking collectives  51 us (23%)
  local copies, waits for them, and re-layouts  18.9 us (8%)
  other arithmetic  14.8 us (7%)
  matrix products  9.18 us (4%)
    ppermute x8, waiting for transfers between devices, shift(): return lax.ppermute(x, axis, [(i, (i + k) % n) for i in range(n)])  49.8 us
    ppermute x9, starting transfers between devices, flip(): return lax.ppermute(x, axis, [(i, i ^ bit) for i in range(n)])  34.5 us
    ppermute x9, waiting for transfers between devices, flip(): return lax.ppermute(x, axis, [(i, i ^ bit) for i in range(n)])  19 us
    all_gather x1, blocking collectives, on_device(): packed = lax.all_gather(packed, 'z', axis=0, tiled=True)  18.8 us
    all_gather x1, blocking collectives, on_device(): lax.all_gather(part, 'z', axis=0, tiled=True).reshape(half, depth, rank)  18.6 us
    all_to_all x1, blocking collectives, scatter_exchange(): lax.all_to_all(parts, axis, split_axis=0, concat_axis=0)  13.6 us
    ppermute x8, starting transfers between devices, shift(): return lax.ppermute(x, axis, [(i, (i + k) % n) for i in range(n)])  11 us
    all_to_all x1, starting transfers between devices, scatter_exchange(): lax.all_to_all(parts, axis, split_axis=0, concat_axis=0)  8.19 us
  transfers between devices with their start and end apart: 18, of which 15 were waited for; matrix products, arithmetic and copies ran while one was open for 5% of the time, Pallas kernels for 0%

commit v1 on v0

--- a/solution.py
+++ b/solution.py
@@ -1,12 +1,23 @@
+import functools
 import jax
 import jax.numpy as jnp
 from jax import lax
 from jax.sharding import Mesh, PartitionSpec as P
+from jax.lax import all_to_all, axis_size
 
 ADAM_STEP = 100
 HIGH = lax.Precision.HIGHEST
 SIZES = {"z": 8, "y": 4, "xh": 2, "core": 2, "xl": 2}
 REP = ("z", "y", "xh", "core")
+
+
+def _enter_row(vector, which_axis):
+    formed = all_to_all(jnp.stack([vector] * axis_size(which_axis), 0), which_axis, 0, 0)
+    current_block = jnp.concatenate(formed, 0)
+    return current_block
+
+
+match_orders_over_axis = functools.partial(_enter_row, which_axis="z")
 
 
 def shift(x, axis, k):
@@ -94,7 +105,7 @@
     part = part + flip(part, "y", 1)
     part = part + flip(part, "y", 2)
     part = part + flip(part, "xh")
-    refresh = lax.all_gather(part, "z", axis=0, tiled=True).reshape(half, depth, rank)
+    refresh = match_orders_over_axis(part).reshape(half, depth, rank)
     gram = jnp.einsum("ldr,lds->lrs", refresh, refresh, precision=HIGH)
     gram = gram + flip(gram, "xl")
     sumsq = jnp.einsum("lrr->l", gram)

time: 225 us -> 199 us (0.88)
  blocking collectives: 51 us -> 30.3 us
  waiting for transfers between devices: 76.2 us -> 70.9 us
    all_gather x1 -> x0, blocking collectives: 18.6 us -> none  [on_device(): lax.all_gather(part, 'z', axis=0, tiled=True).reshape(half, depth, rank)]
    ppermute x9, starting transfers between devices: 34.5 us -> 29.9 us  [flip(): return lax.ppermute(x, axis, [(i, i ^ bit) for i in range(n)])]
    ppermute x8, waiting for transfers between devices: 49.8 us -> 45.2 us  [shift(): return lax.ppermute(x, axis, [(i, (i + k) % n) for i in range(n)])]
    all_to_all x1 -> x2, starting transfers between devices: 8.19 us -> 11.6 us  [scatter_exchange(): lax.all_to_all(parts, axis, split_axis=0, concat_axis=0)]
    all_to_all x1 -> x2, waiting for transfers between devices: 7.36 us -> 7.36 us  [scatter_exchange(): lax.all_to_all(parts, axis, split_axis=0, concat_axis=0)]
  transfers between devices with their start and end apart: 18 -> 19, of which waited for: 15 -> 15; matrix products, arithmetic and copies ran while one was open for 5% -> 6% of each run, Pallas kernels for 0% -> 0%
where the time goes in v1:
time: 199 us; the launch traced here: 198 us
  waiting for transfers between devices  70.9 us (36%)
  starting transfers between devices  52.4 us (26%)
  blocking collectives  30.3 us (15%)
  local copies, waits for them, and re-layouts  18.9 us (9%)
  other arithmetic  14.8 us (7%)
  matrix products  9.87 us (5%)
    ppermute x8, waiting for transfers between devices, shift(): return lax.ppermute(x, axis, [(i, (i + k) % n) for i in range(n)])  45.2 us
    ppermute x9, starting transfers between devices, flip(): return lax.ppermute(x, axis, [(i, i ^ bit) for i in range(n)])  29.9 us
    all_gather x1, blocking collectives, on_device(): packed = lax.all_gather(packed, 'z', axis=0, tiled=True)  18.8 us
    ppermute x9, waiting for transfers between devices, flip(): return lax.ppermute(x, axis, [(i, i ^ bit) for i in range(n)])  18.3 us
    all_to_all x2, starting transfers between devices, scatter_exchange(): lax.all_to_all(parts, axis, split_axis=0, concat_axis=0)  11.6 us
    all_to_all x1, blocking collectives, _enter_row(): all_to_all(jnp.stack([vector] * axis_size(which_axis), 0), which_axis, 0, 0)  11.5 us
    ppermute x8, starting transfers between devices, shift(): return lax.ppermute(x, axis, [(i, (i + k) % n) for i in range(n)])  11 us
    all_to_all x2, waiting for transfers between devices, scatter_exchange(): lax.all_to_all(parts, axis, split_axis=0, concat_axis=0)  7.36 us
  transfers between devices with their start and end apart: 19, of which 15 were waited for; matrix products, arithmetic and copies ran while one was open for 6% of the time, Pallas kernels for 0%

profile of v1, /device:TPU:1, one launch (start us, length us, event | category | flops | bytes accessed | tf_op | source)
XLA Modules:
  0.0 198.1 jit_solution(12746454700547666834)
XLA Ops:
  0.7 1.9 dynamic-slice_bitcast_fusion
  2.5 3.3 %collective-permute-start.1 = (f32[2,192,1536]{2,1,0:T(8,128)S(1)}, f32[2,192,1536]{2,1,0:T(8,128)}, u32[]{:S(2)}, u32[]{:S(2)}) collective-permute-start(f32[2,192,1536]{2,1,0:T(8,128)S(1)} %dynamic-slice_bitcast_fusion), channel_id=1, source_target_pairs={{0,2},{2,0},{1,3},{3,1},{4,6},{6,4},{5,7},{7,5},{8,10},{10,8},{9,1... | collective-permute-start | bytes 7077896 | tf_op jit(solution)/shard_map/ppermute | solution.py:30
  5.9 4.3 %collective-permute-done.1 = f32[2,192,1536]{2,1,0:T(8,128)} collective-permute-done((f32[2,192,1536]{2,1,0:T(8,128)S(1)}, f32[2,192,1536]{2,1,0:T(8,128)}, u32[]{:S(2)}, u32[]{:S(2)}) %collective-permute-start.1) | collective-permute-done | bytes 2359328 | tf_op jit(solution)/shard_map/ppermute | solution.py:30
  10.1 2.8 %bitcast_add_fusion = f32[2,192,1536]{2,1,0:T(8,128)S(1)} fusion(f32[2,192,1536]{2,1,0:T(8,128)} %collective-permute-done.1, f32[1,4,192,1536]{3,2,1,0:T(8,128)} %param.5, s32[]{:T(128)S(6)} %select_n.129), kind=kLoop, calls=%fused_computation.7 | loop fusion | flops 589824 | bytes 7077892 | tf_op jit(solution)/shard_map/add | solution.py:76
  16.1 12.8 %collective-permute-done.4 = f32[384,384]{0,1:T(8,128)} collective-permute-done((f32[384,384]{0,1:T(8,128)}, f32[384,384]{0,1:T(8,128)}, u32[]{:S(2)}, u32[]{:S(2)}) %collective-permute-start.4) | collective-permute-done | bytes 589856 | tf_op jit(solution)/shard_map/ppermute | solution.py:25
  28.9 2.3 %collective-permute-done.3 = f32[384,384]{0,1:T(8,128)} collective-permute-done((f32[384,384]{0,1:T(8,128)}, f32[384,384]{0,1:T(8,128)}, u32[]{:S(2)}, u32[]{:S(2)}) %collective-permute-start.3) | collective-permute-done | bytes 589856 | tf_op jit(solution)/shard_map/ppermute | solution.py:25
  31.2 13.3 %collective-permute-done.2 = f32[384,384]{0,1:T(8,128)} collective-permute-done((f32[384,384]{0,1:T(8,128)S(1)}, f32[384,384]{0,1:T(8,128)}, u32[]{:S(2)}, u32[]{:S(2)}) %collective-permute-start.2) | collective-permute-done | bytes 589856 | tf_op jit(solution)/shard_map/ppermute | solution.py:25
  44.5 1.5 fusion.5
  46.2 2.8 %collective-permute-start.5 = (f32[192,384]{0,1:T(8,128)S(1)}, f32[192,384]{0,1:T(8,128)S(1)}, u32[]{:S(2)}, u32[]{:S(2)}) collective-permute-start(f32[192,384]{0,1:T(8,128)S(1)} %constant_dynamic-slice_fusion), channel_id=1, source_target_pairs={{0,4},{4,0},{1,5},{5,1},{2,6},{6,2},{3,7},{7,3},{8,12},{12,8},{9,1... | collective-permute-start | bytes 884744 | tf_op jit(solution)/shard_map/ppermute | solution.py:25
  50.3 7.6 %collective-permute-done.5 = f32[192,384]{0,1:T(8,128)S(1)} collective-permute-done((f32[192,384]{0,1:T(8,128)S(1)}, f32[192,384]{0,1:T(8,128)S(1)}, u32[]{:S(2)}, u32[]{:S(2)}) %collective-permute-start.5) | collective-permute-done | bytes 294944 | tf_op jit(solution)/shard_map/ppermute | solution.py:25
  58.9 8.2 %all-to-all-start = ((f32[8,24,384]{2,1,0:T(8,128)}), f32[8,24,384]{2,1,0:T(8,128)S(1)}, u32[]{:S(2)}, u32[]{:S(2)}) async-start(f32[8,24,384]{2,1,0:T(8,128)} %bitcast.9), calls=%async_computation | async-start | bytes 589824 | tf_op jit(solution)/shard_map/all_to_all | solution.py:64
  68.4 1.5 collective-permute-done
  70.0 7.4 %all-to-all-done = f32[8,24,384]{2,1,0:T(8,128)S(1)} async-done(((f32[8,24,384]{2,1,0:T(8,128)}), f32[8,24,384]{2,1,0:T(8,128)S(1)}, u32[]{:S(2)}, u32[]{:S(2)}) %all-to-all-start) | async-done | bytes 294944 | tf_op jit(solution)/shard_map/all_to_all | solution.py:64
  80.8 18.8 %all_gather.3 = f32[192,384]{1,0:T(8,128)S(1)} all-gather(f32[24,384]{1,0:T(8,128)S(1)} %pad_maximum_fusion.3), channel_id=1, replica_groups=mesh['z'=8,'y'=4,'xh'=2,'core'=2,'xl'=2] {'z'}, dimensions={0}, use_global_device_ids=true | all-gather | bytes 331776 | tf_op jit(solution)/shard_map/all_gather | solution.py:117
  99.6 2.7 %collective-permute-start.7 = (f32[192,384]{1,0:T(8,128)S(1)}, f32[192,384]{1,0:T(8,128)S(1)}, u32[]{:S(2)}, u32[]{:S(2)}) collective-permute-start(f32[192,384]{1,0:T(8,128)S(1)} %all_gather.3), channel_id=1, source_target_pairs={{0,4},{4,0},{1,5},{5,1},{2,6},{6,2},{3,7},{7,3},{8,12},{12,8},{9,1... | collective-permute-start | bytes 884744 | tf_op jit(solution)/shard_map/ppermute | solution.py:25
  102.5 3.5 %dynamic_update_slice.18 = f32[384,384]{0,1:T(8,128)S(1)} dynamic-update-slice(f32[384,384]{0,1:T(8,128)S(1)} %broadcast_in_dim.15, f32[192,384]{0,1:T(8,128)S(1)} %copy.23, s32[]{:T(128)S(6)} %select_n.141, s32[]{:T(128)} %constant.94.clone.1) | dynamic-update-slice | bytes 589828 | tf_op jit(solution)/shard_map/dynamic_update_slice | solution.py:55
  106.8 3.4 %dynamic_update_slice.19 = f32[384,384]{0,1:T(8,128)S(1)} dynamic-update-slice(f32[384,384]{0,1:T(8,128)S(1)} %dynamic_update_slice.18, f32[192,384]{0,1:T(8,128)S(1)} %copy.24, s32[]{:T(128)S(6)} %select_n.147, s32[]{:T(128)} %constant.94.clone.1) | dynamic-update-slice | bytes 589828 | tf_op jit(solution)/shard_map/dynamic_update_slice | solution.py:57
  111.6 2.0 collective-permute-start.10
  114.8 3.4 %all-to-all-start.1 = ((f32[8,48,128]{2,1,0:T(8,128)}), f32[8,48,128]{2,1,0:T(8,128)S(1)}, u32[]{:S(2)}, u32[]{:S(2)}) async-start(f32[8,48,128]{2,1,0:T(8,128)} %bitcast.23), calls=%async_computation.1 | async-start | bytes 393216 | tf_op jit(solution)/shard_map/all_to_all | solution.py:64
  118.5 8.7 %collective-permute-done.8 = f32[384,384]{0,1:T(8,128)} collective-permute-done((f32[384,384]{0,1:T(8,128)S(1)}, f32[384,384]{0,1:T(8,128)}, u32[]{:S(2)}, u32[]{:S(2)}) %collective-permute-start.8) | collective-permute-done | bytes 589856 | tf_op jit(solution)/shard_map/ppermute | solution.py:25
  130.7 13.0 %collective-permute-start.11 = (f32[1536,384]{0,1:T(8,128)S(1)}, f32[1536,384]{0,1:T(8,128)}, u32[]{:S(2)}, u32[]{:S(2)}) collective-permute-start(f32[1536,384]{0,1:T(8,128)S(1)} %constant_dynamic-update-slice_fusion), channel_id=1, source_target_pairs={{0,2},{2,0},{1,3},{3,1},{4,6},{6,4},{5,7},{7,5},{8,10},{10,8},{9,1... | collective-permute-start | bytes 7077896 | tf_op jit(solution)/shard_map/ppermute | solution.py:30
  143.8 2.7 %collective-permute-done.12 = f32[48,128]{1,0:T(8,128)S(1)} collective-permute-done((f32[48,128]{1,0:T(8,128)S(1)}, f32[48,128]{1,0:T(8,128)S(1)}, u32[]{:S(2)}, u32[]{:S(2)}) %collective-permute-start.12) | collective-permute-done | bytes 24608 | tf_op jit(solution)/shard_map/ppermute | solution.py:30
  147.2 3.4 %collective-permute-done.13 = f32[48,128]{1,0:T(8,128)S(1)} collective-permute-done((f32[48,128]{1,0:T(8,128)S(1)}, f32[48,128]{1,0:T(8,128)S(1)}, u32[]{:S(2)}, u32[]{:S(2)}) %collective-permute-start.13) | collective-permute-done | bytes 24608 | tf_op jit(solution)/shard_map/ppermute | solution.py:30
  150.7 2.8 %collective-permute-start.14 = (f32[48,128]{1,0:T(8,128)S(1)}, f32[48,128]{1,0:T(8,128)S(1)}, u32[]{:S(2)}, u32[]{:S(2)}) collective-permute-start(f32[48,128]{1,0:T(8,128)S(1)} %add.190), channel_id=1, source_target_pairs={{0,4},{4,0},{1,5},{5,1},{2,6},{6,2},{3,7},{7,3},{8,12},{12,8},{9,1... | collective-permute-start | bytes 73736 | tf_op jit(solution)/shard_map/ppermute | solution.py:30
  154.9 11.5 %all_to_all.15 = f32[8,48,128]{2,1,0:T(8,128)S(1)} all-to-all(f32[8,48,128]{2,1,0:T(8,128)S(1)} %stack.11), channel_id=1, replica_groups=mesh['z'=8,'y'=4,'xh'=2,'core'=2,'xl'=2] {'z'}, dimensions={0} | all-to-all | bytes 393216 | tf_op jit(solution)/shard_map/all_to_all | solution.py:15
  168.4 2.6 %collective-permute-done.15 = f32[2,128,128]{2,1,0:T(8,128)S(1)} collective-permute-done((f32[2,128,128]{2,1,0:T(8,128)S(1)}, f32[2,128,128]{2,1,0:T(8,128)S(1)}, u32[]{:S(2)}, u32[]{:S(2)}) %collective-permute-start.15) | collective-permute-done | bytes 131104 | tf_op jit(solution)/shard_map/ppermute | solution.py:30
  171.5 6.0 %collective-permute-start.16 = (f32[2,192,128]{2,1,0:T(8,128)S(1)}, f32[2,192,128]{2,1,0:T(8,128)S(1)}, u32[]{:S(2)}, u32[]{:S(2)}) collective-permute-start(f32[2,192,128]{2,1,0:T(8,128)S(1)} %fusion.3), channel_id=1, source_target_pairs={{0,2},{2,0},{1,3},{3,1},{4,6},{6,4},{5,7},{7,5},{8,10},{10,8},{9,1... | collective-permute-start | bytes 589832 | tf_op jit(solution)/shard_map/ppermute | solution.py:30
  179.5 2.1 %select_bitcast_fusion = (f32[1,1536,384]{1,2,0:T(8,128)S(1)}, f32[1,1536,384]{1,2,0:T(8,128)S(1)}) fusion(f32[1536,384]{0,1:T(8,128)} %collective-permute-done.11, f32[1536,384]{0,1:T(8,128)S(1)} %constant_dynamic-update-slice_fusion, pred[]{:T(512)S(6)} %eq.20), kind=kLoop, calls=%fused_computation.8 | loop fusion | flops 1179648 | bytes 9437185 | tf_op jit(solution)/shard_map/stack | solution.py:120
  181.6 1.7 pad_maximum_fusion.1
  183.5 2.4 %copy.25 = f32[2,3072,128]{2,1,0:T(8,128)} copy(f32[2,3072,128]{1,2,0:T(8,128)S(1)} %pad_maximum_fusion) | data formatting | bytes 6291456 | tf_op jit(solution)/shard_map/concatenate
  185.9 4.9 %fusion = (f32[4,64,1536]{2,1,0:T(8,128)}, f32[4,64,1536]{2,1,0:T(8,128)}) fusion(f32[4,64,1536]{2,1,0:T(8,128)} %bitcast.50, f32[4,64,1536]{2,1,0:T(8,128)} %param.9, f32[4,64,1536]{2,1,0:T(8,128)} %param.8), kind=kLoop, calls=%fused_computation.11 | loop fusion | flops 2752512 | bytes 7864320 | tf_op jit(solution)/shard_map/add | solution.py:125
  190.8 7.3 %bitcast_subtract_fusion = f32[4,192,1536]{2,1,0:T(8,128)} fusion(f32[4,192,1536]{2,1,0:T(8,128)} %param.7, f32[4,1536,128]{2,1,0:T(8,128)S(1)} %bitcast.47, f32[4,192,128]{2,1,0:T(8,128)S(1)} %copy-done), kind=kOutput, calls=%fused_computation.4 | convolution fusion | flops 1814298624 | bytes 12976128 | tf_op jit(solution)/shard_map/ldr,lfr->ldf/dot_general | solution.py:127
  (63 shorter events, 24.7 us)
Async XLA Ops:
  0.6 76.8 %copy-start = (f32[4,192,128]{2,1,0:T(8,128)S(1)}, f32[4,192,128]{2,1,0:T(8,128)}, u32[]{:S(2)}) copy-start(f32[4,192,128]{2,1,0:T(8,128)} %param.6) | copy-start | bytes 1179652
  2.5 7.6 %collective-permute-start.1 = (f32[2,192,1536]{2,1,0:T(8,128)S(1)}, f32[2,192,1536]{2,1,0:T(8,128)}, u32[]{:S(2)}, u32[]{:S(2)}) collective-permute-start(f32[2,192,1536]{2,1,0:T(8,128)S(1)} %dynamic-slice_bitcast_fusion), channel_id=1, source_target_pairs={{0,2},{2,0},{1,3},{3,1},{4,6},{6,4},{5,7},{7,5},{8,10},{10,8},{9,1... | collective-permute-start | bytes 7077896 | tf_op jit(solution)/shard_map/ppermute | solution.py:30
  14.1 14.9 %collective-permute-start.4 = (f32[384,384]{0,1:T(8,128)}, f32[384,384]{0,1:T(8,128)}, u32[]{:S(2)}, u32[]{:S(2)}) collective-permute-start(f32[384,384]{0,1:T(8,128)} %get-tuple-element.16), channel_id=1, source_target_pairs={{0,24},{8,0},{16,8},{24,16},{1,25},{9,1},{17,9},{25,17},{2,26},{10... | collective-permute-start | bytes 1769480 | tf_op jit(solution)/shard_map/ppermute | solution.py:25
  15.1 16.1 %collective-permute-start.3 = (f32[384,384]{0,1:T(8,128)}, f32[384,384]{0,1:T(8,128)}, u32[]{:S(2)}, u32[]{:S(2)}) collective-permute-start(f32[384,384]{0,1:T(8,128)} %get-tuple-element.17), channel_id=1, source_target_pairs={{0,16},{8,24},{16,0},{24,8},{1,17},{9,25},{17,1},{25,9},{2,18},{10... | collective-permute-start | bytes 1769480 | tf_op jit(solution)/shard_map/ppermute | solution.py:25
  15.4 29.0 %collective-permute-start.2 = (f32[384,384]{0,1:T(8,128)S(1)}, f32[384,384]{0,1:T(8,128)}, u32[]{:S(2)}, u32[]{:S(2)}) collective-permute-start(f32[384,384]{0,1:T(8,128)S(1)} %get-tuple-element.15), channel_id=1, source_target_pairs={{0,8},{8,16},{16,24},{24,0},{1,9},{9,17},{17,25},{25,1},{2,10},{10... | collective-permute-start | bytes 1769480 | tf_op jit(solution)/shard_map/ppermute | solution.py:25
  46.2 11.6 %collective-permute-start.5 = (f32[192,384]{0,1:T(8,128)S(1)}, f32[192,384]{0,1:T(8,128)S(1)}, u32[]{:S(2)}, u32[]{:S(2)}) collective-permute-start(f32[192,384]{0,1:T(8,128)S(1)} %constant_dynamic-slice_fusion), channel_id=1, source_target_pairs={{0,4},{4,0},{1,5},{5,1},{2,6},{6,2},{3,7},{7,3},{8,12},{12,8},{9,1... | collective-permute-start | bytes 884744 | tf_op jit(solution)/shard_map/ppermute | solution.py:25
  58.9 18.5 %all-to-all-start = ((f32[8,24,384]{2,1,0:T(8,128)}), f32[8,24,384]{2,1,0:T(8,128)S(1)}, u32[]{:S(2)}, u32[]{:S(2)}) async-start(f32[8,24,384]{2,1,0:T(8,128)} %bitcast.9), calls=%async_computation | async-start | bytes 589824 | tf_op jit(solution)/shard_map/all_to_all | solution.py:64
  67.1 2.7 %collective-permute-start = (f32[2,24,128]{2,1,0:T(8,128)S(1)}, f32[2,24,128]{2,1,0:T(8,128)S(1)}, u32[]{:S(2)}, u32[]{:S(2)}) collective-permute-start(f32[2,24,128]{2,1,0:T(8,128)S(1)} %pad_maximum_fusion.4), channel_id=1, source_target_pairs={{0,1},{1,0},{2,3},{3,2},{4,5},{5,4},{6,7},{7,6},{8,9},{9,8},{10,11... | collective-permute-start | bytes 73736 | tf_op jit(solution)/shard_map/ppermute | solution.py:30
  77.8 2.8 %collective-permute-start.6 = (f32[2,24,128]{2,1,0:T(8,128)S(1)}, f32[2,24,128]{2,1,0:T(8,128)S(1)}, u32[]{:S(2)}, u32[]{:S(2)}) collective-permute-start(f32[2,24,128]{2,1,0:T(8,128)S(1)} %fusion.7), channel_id=1, source_target_pairs={{0,1},{1,0},{2,3},{3,2},{4,5},{5,4},{6,7},{7,6},{8,9},{9,8},{10,11... | collective-permute-start | bytes 73736 | tf_op jit(solution)/shard_map/ppermute | solution.py:30
  99.6 7.1 %collective-permute-start.7 = (f32[192,384]{1,0:T(8,128)S(1)}, f32[192,384]{1,0:T(8,128)S(1)}, u32[]{:S(2)}, u32[]{:S(2)}) collective-permute-start(f32[192,384]{1,0:T(8,128)S(1)} %all_gather.3), channel_id=1, source_target_pairs={{0,4},{4,0},{1,5},{5,1},{2,6},{6,2},{3,7},{7,3},{8,12},{12,8},{9,1... | collective-permute-start | bytes 884744 | tf_op jit(solution)/shard_map/ppermute | solution.py:25
  110.2 17.0 %collective-permute-start.8 = (f32[384,384]{0,1:T(8,128)S(1)}, f32[384,384]{0,1:T(8,128)}, u32[]{:S(2)}, u32[]{:S(2)}) collective-permute-start(f32[384,384]{0,1:T(8,128)S(1)} %dynamic_update_slice.19), channel_id=1, source_target_pairs={{0,8},{8,16},{16,24},{24,0},{1,9},{9,17},{17,25},{25,1},{2,10},{10... | collective-permute-start | bytes 1769480 | tf_op jit(solution)/shard_map/ppermute | solution.py:25
  110.3 18.1 %collective-permute-start.9 = (f32[384,384]{0,1:T(8,128)S(1)}, f32[384,384]{0,1:T(8,128)}, u32[]{:S(2)}, u32[]{:S(2)}) collective-permute-start(f32[384,384]{0,1:T(8,128)S(1)} %dynamic_update_slice.19), channel_id=1, source_target_pairs={{0,16},{8,24},{16,0},{24,8},{1,17},{9,25},{17,1},{25,9},{2,18},{10... | collective-permute-start | bytes 1769480 | tf_op jit(solution)/shard_map/ppermute | solution.py:25
  111.6 17.9 %collective-permute-start.10 = (f32[384,384]{0,1:T(8,128)S(1)}, f32[384,384]{0,1:T(8,128)}, u32[]{:S(2)}, u32[]{:S(2)}) collective-permute-start(f32[384,384]{0,1:T(8,128)S(1)} %dynamic_update_slice.19), channel_id=1, source_target_pairs={{0,24},{8,0},{16,8},{24,16},{1,25},{9,1},{17,9},{25,17},{2,26},{10... | collective-permute-start | bytes 1769480 | tf_op jit(solution)/shard_map/ppermute | solution.py:25
  114.8 28.9 %all-to-all-start.1 = ((f32[8,48,128]{2,1,0:T(8,128)}), f32[8,48,128]{2,1,0:T(8,128)S(1)}, u32[]{:S(2)}, u32[]{:S(2)}) async-start(f32[8,48,128]{2,1,0:T(8,128)} %bitcast.23), calls=%async_computation.1 | async-start | bytes 393216 | tf_op jit(solution)/shard_map/all_to_all | solution.py:64
  130.7 48.8 %collective-permute-start.11 = (f32[1536,384]{0,1:T(8,128)S(1)}, f32[1536,384]{0,1:T(8,128)}, u32[]{:S(2)}, u32[]{:S(2)}) collective-permute-start(f32[1536,384]{0,1:T(8,128)S(1)} %constant_dynamic-update-slice_fusion), channel_id=1, source_target_pairs={{0,2},{2,0},{1,3},{3,1},{4,6},{6,4},{5,7},{7,5},{8,10},{10,8},{9,1... | collective-permute-start | bytes 7077896 | tf_op jit(solution)/shard_map/ppermute | solution.py:30
  143.7 2.8 %collective-permute-start.12 = (f32[48,128]{1,0:T(8,128)S(1)}, f32[48,128]{1,0:T(8,128)S(1)}, u32[]{:S(2)}, u32[]{:S(2)}) collective-permute-start(f32[48,128]{1,0:T(8,128)S(1)} %reduce_sum.28), channel_id=1, source_target_pairs={{0,8},{8,0},{16,24},{24,16},{1,9},{9,1},{17,25},{25,17},{2,10},{10... | collective-permute-start | bytes 73736 | tf_op jit(solution)/shard_map/ppermute | solution.py:30
  146.5 4.2 %collective-permute-start.13 = (f32[48,128]{1,0:T(8,128)S(1)}, f32[48,128]{1,0:T(8,128)S(1)}, u32[]{:S(2)}, u32[]{:S(2)}) collective-permute-start(f32[48,128]{1,0:T(8,128)S(1)} %add.189), channel_id=1, source_target_pairs={{0,16},{8,24},{16,0},{24,8},{1,17},{9,25},{17,1},{25,9},{2,18},{10... | collective-permute-start | bytes 73736 | tf_op jit(solution)/shard_map/ppermute | solution.py:30
  150.7 4.2 %collective-permute-start.14 = (f32[48,128]{1,0:T(8,128)S(1)}, f32[48,128]{1,0:T(8,128)S(1)}, u32[]{:S(2)}, u32[]{:S(2)}) collective-permute-start(f32[48,128]{1,0:T(8,128)S(1)} %add.190), channel_id=1, source_target_pairs={{0,4},{4,0},{1,5},{5,1},{2,6},{6,2},{3,7},{7,3},{8,12},{12,8},{9,1... | collective-permute-start | bytes 73736 | tf_op jit(solution)/shard_map/ppermute | solution.py:30
  167.1 3.9 %collective-permute-start.15 = (f32[2,128,128]{2,1,0:T(8,128)S(1)}, f32[2,128,128]{2,1,0:T(8,128)S(1)}, u32[]{:S(2)}, u32[]{:S(2)}) collective-permute-start(f32[2,128,128]{2,1,0:T(8,128)S(1)} %fusion.26), channel_id=1, source_target_pairs={{0,1},{1,0},{2,3},{3,2},{4,5},{5,4},{6,7},{7,6},{8,9},{9,8},{10,11... | collective-permute-start | bytes 393224 | tf_op jit(solution)/shard_map/ppermute | solution.py:30
  171.5 7.1 %collective-permute-start.16 = (f32[2,192,128]{2,1,0:T(8,128)S(1)}, f32[2,192,128]{2,1,0:T(8,128)S(1)}, u32[]{:S(2)}, u32[]{:S(2)}) collective-permute-start(f32[2,192,128]{2,1,0:T(8,128)S(1)} %fusion.3), channel_id=1, source_target_pairs={{0,2},{2,0},{1,3},{3,1},{4,6},{6,4},{5,7},{7,5},{8,10},{10,8},{9,1... | collective-permute-start | bytes 589832 | tf_op jit(solution)/shard_map/ppermute | solution.py:30
  185.9 4.9 %copy-start.1 = (f32[2,3072,128]{2,1,0:T(8,128)S(1)}, f32[2,3072,128]{2,1,0:T(8,128)}, u32[]{:S(2)}) copy-start(f32[2,3072,128]{2,1,0:T(8,128)} %copy.25) | copy-start | bytes 9437188
